TPU v7x, 256 devices: a whole 4x4x8 slice. The times are simulated.
256 devices in a mesh: light: 4 (over x), view: 64 (over y, z, core).
Axes of the slice: x: 4, y: 4, z: 8, core: 2. Of those that a mesh axis runs over, the one named last changes fastest.
Arguments:
- density: float32 [512, 256, 4096], P('view', 'light'), may hold values from 0 to 1
- tables: float32 [8, 4, 16], replicated, may hold values from 0.2 to 2
- table_index: int32 [4, 64], P('light', 'view'), may hold values from 0 to 7
- light_code: int32 [4], replicated, may hold values from -1 to 1, as said below
- light_tint: float32 [4, 3], replicated, may hold values from 0.25 to 1
Outputs:
- image: float32 [4, 256, 4096], P(None, ('light', 'view'))
Inputs may be any that keep to these rules, and one draw needn't show every extreme that they name: `light_code`: each of -1, 0 and 1 occurs.
All inputs are finite; a program needn't handle non-finite values.
Results may differ from a plain program's by a relative error of at most 0.0003.
Values sent between devices are 32-bit elements; how exact they have to be, the bound alone decides.
A program may use at most 256 MiB of HBM per device.

v0:
```python
import functools
import math

import jax
import jax.numpy as jnp
from jax import lax
from jax.experimental import pallas as pl
from jax.experimental.pallas import tpu as pltpu
from jax.sharding import PartitionSpec as P

MESH = pl.DeviceIdType.MESH
LANES = 128
SUB = 8
NZ, NCORE = 8, 2


def lookup(row, index):
    return jnp.take_along_axis(row, index, axis=1, mode="promise_in_bounds")


def over(front, back):
    out = [front[k] + front[3] * back[k] for k in range(3)]
    return out + [front[3] * back[3]]


def kernel(
    nx, ny, layers, slices, columns, knots, table_count, lights,
    index_ref, code_ref, tint_ref, tables_ref, density_ref, out_ref,
    dens, keep, tab, leave, leave_in, fronts, light, part, core_in, z_in, y_part, y_in,
    dens_sem, leave_send, leave_recv, core_send, core_recv, z_send, z_recv, y_send, y_recv,
):
    x = lax.axis_index("light")
    v = lax.axis_index("view")
    core = v % NCORE
    z = (v // NCORE) % NZ
    y = v // (NCORE * NZ)
    blocks = columns // (SUB * LANES)
    tiles_a = slices // SUB
    tiles = columns // LANES

    def at_view(yy, zz, cc):
        return {"view": (yy * NZ + zz) * NCORE + cc}

    for block in range(blocks):
        pltpu.make_async_copy(
            density_ref.at[:, :, pl.ds(block * SUB * SUB, SUB * SUB)], dens.at[block], dens_sem.at[block]
        ).start()

    barrier = pltpu.get_barrier_semaphore()
    peers = [at_view(y, z, 1 - core)]
    peers += [at_view(y, (z + d) % NZ, core) for d in range(1, NZ)]
    peers += [at_view((y + d) % ny, z, core) for d in range(1, ny)]
    peers += [{"light": (x + d) % nx} for d in range(1, nx)]
    for peer in peers:
        pl.semaphore_signal(barrier, inc=1, device_id=peer, device_id_type=MESH)

    chosen = tables_ref[index_ref[0, 0]]
    tab[...] = jnp.zeros_like(tab)
    tab[0:4, 0:knots] = chosen
    knot_values = tab[...]
    lane = lax.broadcasted_iota(jnp.int32, (SUB, LANES), 1)
    rise = jnp.where(lane < knots - 1, pltpu.roll(knot_values, LANES - 1, 1) - knot_values, 0.0)
    base = knot_values - rise * lane.astype(jnp.float32)
    slope = rise * float(knots - 1)
    depth_scale = -math.log2(math.e) * math.exp2(-9)
    rows = []
    for q in range(4):
        scale = depth_scale if q == 0 else 1.0
        rows.append(
            tuple(jnp.broadcast_to(t[q : q + 1] * scale, (SUB, LANES)) for t in (base, slope))
        )

    def cell_index(d):
        return (d * float(knots - 1)).astype(jnp.int32)

    for block in range(blocks):
        pltpu.make_async_copy(dens.at[block], dens.at[block], dens_sem.at[block]).wait()

        def first(tile, sums, block=block):
            sums = list(sums)
            for row in range(SUB):
                for b in range(layers):
                    d = dens[block, b, tile, pl.ds(row, SUB, stride=SUB), :]
                    k = cell_index(d)
                    depth = lookup(rows[0][0], k) + lookup(rows[0][1], k) * d
                    keep[block, tile * SUB + row, b] = jnp.exp2(depth)
                    sums[b] = sums[b] + depth
            return tuple(sums)

        zero = jnp.zeros((SUB, LANES), jnp.float32)
        sums = lax.fori_loop(0, tiles_a, first, (zero,) * layers)
        for b in range(layers):
            leave[block, pl.ds(b * SUB, SUB)] = jnp.exp2(sums[b] * 2.0)
        if block == 0:
            pl.semaphore_wait(barrier, len(peers))
        for d in range(1, nx):

            @pl.when(x + d < nx)
            def _(d=d, block=block):
                pltpu.make_async_remote_copy(
                    src_ref=leave.at[block], dst_ref=leave_in.at[x, block],
                    send_sem=leave_send.at[d, block], recv_sem=leave_recv.at[x, block],
                    device_id={"light": (x + d) % nx}, device_id_type=MESH,
                ).start()

    column = lax.broadcasted_iota(jnp.int32, (layers, columns), 1)
    fronts[...] = jnp.ones_like(fronts)

    def moved(values, by):
        rolled = pltpu.roll(values, by % columns, 1)
        inside = column >= by if by > 0 else column < columns + by
        return jnp.where(inside, rolled, 0.0)

    for stage in range(nx - 1):

        @pl.when(x > stage)
        def _(stage=stage):
            for block in range(blocks):
                pltpu.make_async_copy(
                    leave_in.at[stage, block], leave_in.at[stage, block], leave_recv.at[stage, block]
                ).wait()
            gone = jnp.concatenate(
                [leave_in[stage, t // SUB, pl.ds(t % SUB, layers, stride=SUB), :] for t in range(tiles)], axis=1
            )
            for drift in (-1, 0, 1):
                value = fronts[drift + 1] * gone
                total = 0.0
                for offset, share in ((drift - 1, 0.25), (drift, 0.5), (drift + 1, 0.25)):
                    total = total + share * (moved(value, offset) if offset else value)
                fronts[drift + 1] = total

    for k in range(3):
        tint = [0.0, 0.0, 0.0]
        for l in range(lights):
            for drift in (-1, 0, 1):
                tint[drift + 1] = tint[drift + 1] + jnp.where(code_ref[l] == drift, tint_ref[l, k], 0.0)
        for t in range(tiles):
            cols = pl.ds(t * LANES, LANES)
            light[k, t // SUB, pl.ds(t % SUB, layers, stride=SUB), :] = (
                fronts[0, :, cols] * tint[0] + fronts[1, :, cols] * tint[1] + fronts[2, :, cols] * tint[2]
            )

    def core_copy(block):
        return pltpu.make_async_remote_copy(
            src_ref=part.at[block, 1 - core], dst_ref=core_in.at[block],
            send_sem=core_send.at[block], recv_sem=core_recv.at[block],
            device_id=at_view(y, z, 1 - core), device_id_type=MESH,
        )

    def z_copy(block, d):
        to = (z + d) % NZ
        return pltpu.make_async_remote_copy(
            src_ref=part.at[block, core, to], dst_ref=z_in.at[block, z],
            send_sem=z_send.at[block, d], recv_sem=z_recv.at[block, z],
            device_id=at_view(y, to, core), device_id_type=MESH,
        )

    def y_copy(block, d):
        to = (y + d) % ny
        return pltpu.make_async_remote_copy(
            src_ref=y_part.at[block, to], dst_ref=y_in.at[block, y],
            send_sem=y_send.at[block, d], recv_sem=y_recv.at[block, y],
            device_id=at_view(to, z, core), device_id_type=MESH,
        )

    z_order = (4, 1, 7, 2, 6, 3, 5)

    def join_cores(block):
        core_copy(block).wait_recv()

        def join(zz):
            for yy in range(ny):
                mine = [part[block, core, zz, yy, k] for k in range(4)]
                other = [core_in[block, zz, yy, k] for k in range(4)]
                front = [jnp.where(core == 0, m, o) for m, o in zip(mine, other)]
                back = [jnp.where(core == 0, o, m) for m, o in zip(mine, other)]
                joined = over(front, back)
                for k in range(4):
                    part[block, core, zz, yy, k] = joined[k]

        @pl.loop(0, NZ)
        def _(zz):
            join(zz)

        for d in z_order:
            z_copy(block, d).start()
        for yy in range(ny):
            for k in range(4):
                z_in[block, z, yy, k] = part[block, core, z, yy, k]

    for block in range(blocks):

        def second(tile, shadow, block=block):
            shadow = list(shadow)
            for row in range(SUB):
                clear = None
                total = [None] * 3
                for b in range(layers):
                    d = dens[block, b, tile, pl.ds(row, SUB, stride=SUB), :]
                    k = cell_index(d)
                    stays = keep[block, tile * SUB + row, b]
                    if clear is None:
                        weight = (1.0 - stays) * shadow[b]
                        clear = stays
                    else:
                        after = clear * stays
                        weight = (clear - after) * shadow[b]
                        clear = after
                    shadow[b] = shadow[b] * (stays * stays)
                    for c in range(3):
                        color = lookup(rows[c + 1][0], k) + lookup(rows[c + 1][1], k) * d
                        term = color * (weight * light[c, block, pl.ds(b * SUB, SUB), :])
                        total[c] = term if total[c] is None else total[c] + term
                zz = (tile % 2) * (SUB // NCORE) + row // NCORE
                for c in range(3):
                    part[block, row % NCORE, zz, tile // 2, c] = total[c]
                part[block, row % NCORE, zz, tile // 2, 3] = clear
            return tuple(shadow)

        one = jnp.ones((SUB, LANES), jnp.float32)
        lax.fori_loop(0, tiles_a, second, (one,) * layers)
        core_copy(block).start()
        if block:
            join_cores(block - 1)
    join_cores(blocks - 1)

    for block in range(blocks):
        for i in range(1, NZ):
            zz = (z + i) % NZ
            pltpu.make_async_copy(z_in.at[block, zz], z_in.at[block, zz], z_recv.at[block, zz]).wait()

        @pl.loop(0, ny)
        def _(yy):
            total = [z_in[block, 0, yy, k] for k in range(4)]
            for i in range(1, NZ):
                total = over(total, [z_in[block, i, yy, k] for k in range(4)])
            for k in range(4):
                y_part[block, yy, k] = total[k]

        for d in range(1, ny):
            y_copy(block, d).start()
        for k in range(4):
            y_in[block, y, k] = y_part[block, y, k]

    for block in range(blocks):
        for i in range(1, ny):
            yy = (y + i) % ny
            pltpu.make_async_copy(y_in.at[block, yy], y_in.at[block, yy], y_recv.at[block, yy]).wait()
        total = [y_in[block, 0, k] for k in range(4)]
        for i in range(1, ny):
            total = over(total, [y_in[block, i, k] for k in range(4)])
        for k in range(4):
            out_ref[k, pl.ds(block * SUB, SUB)] = total[k]

    for block in range(blocks):
        for d in range(1, nx):

            @pl.when(x + d < nx)
            def _(d=d, block=block):
                pltpu.make_async_copy(leave.at[block], leave.at[block], leave_send.at[d, block]).wait()

        core_copy(block).wait_send()
        for d in range(1, NZ):
            z_copy(block, d).wait_send()
        for d in range(1, ny):
            y_copy(block, d).wait_send()


def local(density, tables, table_index, light_code, light_tint):
    layers, slices, columns = density.shape
    nx, ny = lax.axis_size("light"), lax.axis_size("view") // (NZ * NCORE)
    table_count, _, knots = tables.shape
    tiles = columns // LANES
    blocks = tiles // SUB
    tiled = density.reshape(layers, slices // SUB, SUB, tiles, LANES).transpose(0, 1, 3, 2, 4)
    tiled = tiled.reshape(layers, slices // SUB, tiles * SUB, LANES)
    f32 = jnp.float32
    image = pl.pallas_call(
        functools.partial(kernel, nx, ny, layers, slices, columns, knots, table_count, light_code.shape[0]),
        out_shape=jax.ShapeDtypeStruct((4, tiles, LANES), f32),
        in_specs=[pl.BlockSpec(memory_space=pltpu.SMEM)] * 3
        + [pl.BlockSpec(memory_space=pltpu.VMEM), pl.BlockSpec(memory_space=pl.ANY)],
        out_specs=pl.BlockSpec(memory_space=pltpu.VMEM),
        scratch_shapes=[
            pltpu.VMEM((blocks, layers, slices // SUB, SUB * SUB, LANES), f32),
            pltpu.VMEM((blocks, slices, layers, SUB, LANES), f32),
            pltpu.VMEM((SUB, LANES), f32),
            pltpu.VMEM((blocks, layers * SUB, LANES), f32),
            pltpu.VMEM((nx, blocks, layers * SUB, LANES), f32),
            pltpu.VMEM((3, layers, columns), f32),
            pltpu.VMEM((3, blocks, layers * SUB, LANES), f32),
            pltpu.VMEM((blocks, NCORE, NZ, ny, 4, SUB, LANES), f32),
            pltpu.VMEM((blocks, NZ, ny, 4, SUB, LANES), f32),
            pltpu.VMEM((blocks, NZ, ny, 4, SUB, LANES), f32),
            pltpu.VMEM((blocks, ny, 4, SUB, LANES), f32),
            pltpu.VMEM((blocks, ny, 4, SUB, LANES), f32),
            pltpu.SemaphoreType.DMA((blocks,)),
            pltpu.SemaphoreType.DMA((nx, blocks)),
            pltpu.SemaphoreType.DMA((nx, blocks)),
            pltpu.SemaphoreType.DMA((blocks,)),
            pltpu.SemaphoreType.DMA((blocks,)),
            pltpu.SemaphoreType.DMA((blocks, NZ)),
            pltpu.SemaphoreType.DMA((blocks, NZ)),
            pltpu.SemaphoreType.DMA((blocks, ny)),
            pltpu.SemaphoreType.DMA((blocks, ny)),
        ],
        compiler_params=pltpu.CompilerParams(
            collective_id=0, has_side_effects=True, vmem_limit_bytes=60 * 1024 * 1024
        ),
    )(table_index, light_code, light_tint, tables, tiled)
    return image.reshape(4, 1, columns)


def solution(mesh):
    return jax.shard_map(
        local,
        mesh=mesh,
        in_specs=(P("view", "light", None), P(), P("light", "view"), P(), P()),
        out_specs=P(None, ("light", "view"), None),
        check_vma=False,
    )
```

profile of v0, /device:TPU:6, one launch (start us, length us, event | category | flops | bytes accessed | tf_op | source)
XLA Modules:
  0.0 90.8 jit_solution(14971665511111167398)
XLA Ops:
  0.7 88.7 %shard_map.55 = f32[4,32,128]{2,1,0:T(8,128)} custom-call(s32[1,1]{1,0:T(1,128)S(6)} %copy.8.index_ref, s32[4]{0:T(128)} %code_ref.1, f32[4,3]{1,0:T(4,128)} %tint_ref.1, f32[8,4,16]{2,1,0:T(4,128)} %tables_ref.1, f32[8,8,256,128]{3,2,1,0:T(8,128)} %bitcast.6), custom_call_target="tpu_custom_call" | custom-call | tf_op jit(solution)/shard_map/pallas_call | solution.py:278
  89.4 1.5 %copy.9 = f32[4,1,4096]{2,1,0:T(1,128)} copy(f32[4,1,4096]{2,1,0:T(1,128)} %bitcast.7) | data formatting | bytes 131072
where the time goes:
time: 91 us; the launch traced here: 90.8 us
  Pallas kernels  88.7 us (97%)
  local copies, waits for them, and re-layouts  1.47 us (2%)
    pallas_call x1, Pallas kernels, local(): pl.pallas_call(functools.partial(kernel, nx, ny, layers, slices, columns,...  88.7 us

commit v1 on v0

--- a/solution.py
+++ b/solution.py
@@ -15,7 +15,13 @@
 
 
 def lookup(row, index):
-    return jnp.take_along_axis(row, index, axis=1, mode="promise_in_bounds")
+    numbers = lax.GatherDimensionNumbers(
+        offset_dims=(), collapsed_slice_dims=(1,), start_index_map=(1,),
+        operand_batching_dims=(0,), start_indices_batching_dims=(0,),
+    )
+    return lax.gather(
+        row, index[:, :, None], numbers, (1, 1), mode=lax.GatherScatterMode.PROMISE_IN_BOUNDS
+    )
 
 
 def over(front, back):
@@ -26,8 +32,8 @@
 def kernel(
     nx, ny, layers, slices, columns, knots, table_count, lights,
     index_ref, code_ref, tint_ref, tables_ref, density_ref, out_ref,
-    dens, keep, tab, leave, leave_in, fronts, light, part, core_in, z_in, y_part, y_in,
-    dens_sem, leave_send, leave_recv, core_send, core_recv, z_send, z_recv, y_send, y_recv,
+    dens, cells, knot, keep, tab, leave, leave_in, fronts, light, part, core_in, pair_in, z_in, y_part, y_in,
+    dens_sem, leave_send, leave_recv, core_send, core_recv, pair_send, pair_recv, z_send, z_recv, y_send, y_recv,
 ):
     x = lax.axis_index("light")
     v = lax.axis_index("view")
@@ -84,6 +90,8 @@
                     k = cell_index(d)
                     depth = lookup(rows[0][0], k) + lookup(rows[0][1], k) * d
                     keep[block, tile * SUB + row, b] = jnp.exp2(depth)
+                    cells[block, tile * SUB + row, b] = d
+                    knot[block, tile * SUB + row, b] = k
                     sums[b] = sums[b] + depth
             return tuple(sums)
 
@@ -147,12 +155,26 @@
             device_id=at_view(y, z, 1 - core), device_id_type=MESH,
         )
 
-    def z_copy(block, d):
-        to = (z + d) % NZ
+    pair = z // 2
+    odd = z % 2
+    side = 2 * odd - 1
+    half = NZ // 2
+
+    def owner(j):
+        return (z + side * j + NZ) % NZ
+
+    def pair_copy(block, j):
         return pltpu.make_async_remote_copy(
-            src_ref=part.at[block, core, to], dst_ref=z_in.at[block, z],
-            send_sem=z_send.at[block, d], recv_sem=z_recv.at[block, z],
-            device_id=at_view(y, to, core), device_id_type=MESH,
+            src_ref=part.at[block, core, owner(-1 - j)], dst_ref=pair_in.at[block, j],
+            send_sem=pair_send.at[block, j], recv_sem=pair_recv.at[block, j],
+            device_id=at_view(y, owner(-1), core), device_id_type=MESH,
+        )
+
+    def z_copy(block, j):
+        return pltpu.make_async_remote_copy(
+            src_ref=part.at[block, core, owner(j)], dst_ref=z_in.at[block, pair],
+            send_sem=z_send.at[block, j], recv_sem=z_recv.at[block, pair],
+            device_id=at_view(y, owner(j), core), device_id_type=MESH,
         )
 
     def y_copy(block, d):
@@ -163,30 +185,41 @@
             device_id=at_view(to, z, core), device_id_type=MESH,
         )
 
-    z_order = (4, 1, 7, 2, 6, 3, 5)
+    def ordered(later, mine, other):
+        front = [jnp.where(later, o, m) for m, o in zip(mine, other)]
+        back = [jnp.where(later, m, o) for m, o in zip(mine, other)]
+        return over(front, back)
 
     def join_cores(block):
         core_copy(block).wait_recv()
 
-        def join(zz):
+        @pl.loop(0, NZ)
+        def _(zz):
             for yy in range(ny):
                 mine = [part[block, core, zz, yy, k] for k in range(4)]
                 other = [core_in[block, zz, yy, k] for k in range(4)]
-                front = [jnp.where(core == 0, m, o) for m, o in zip(mine, other)]
-                back = [jnp.where(core == 0, o, m) for m, o in zip(mine, other)]
-                joined = over(front, back)
+                joined = ordered(core == 1, mine, other)
                 for k in range(4):
                     part[block, core, zz, yy, k] = joined[k]
 
-        @pl.loop(0, NZ)
-        def _(zz):
-            join(zz)
-
-        for d in z_order:
-            z_copy(block, d).start()
-        for yy in range(ny):
-            for k in range(4):
-                z_in[block, z, yy, k] = part[block, core, z, yy, k]
+        for j in reversed(range(half)):
+            pair_copy(block, j).start()
+
+    def join_pair(block):
+        for j in reversed(range(half)):
+            pair_copy(block, j).wait_recv()
+            at = owner(j)
+            for yy in range(ny):
+                mine = [part[block, core, at, yy, k] for k in range(4)]
+                other = [pair_in[block, j, yy, k] for k in range(4)]
+                joined = ordered(odd == 1, mine, other)
+                for k in range(4):
+                    if j:
+                        part[block, core, at, yy, k] = joined[k]
+                    else:
+                        z_in[block, pair, yy, k] = joined[k]
+            if j:
+                z_copy(block, j).start()
 
     for block in range(blocks):
 
@@ -196,8 +229,8 @@
                 clear = None
                 total = [None] * 3
                 for b in range(layers):
-                    d = dens[block, b, tile, pl.ds(row, SUB, stride=SUB), :]
-                    k = cell_index(d)
+                    d = cells[block, tile * SUB + row, b]
+                    k = knot[block, tile * SUB + row, b]
                     stays = keep[block, tile * SUB + row, b]
                     if clear is None:
                         weight = (1.0 - stays) * shadow[b]
@@ -225,14 +258,17 @@
     join_cores(blocks - 1)
 
     for block in range(blocks):
-        for i in range(1, NZ):
-            zz = (z + i) % NZ
-            pltpu.make_async_copy(z_in.at[block, zz], z_in.at[block, zz], z_recv.at[block, zz]).wait()
+        join_pair(block)
+
+    for block in range(blocks):
+        for i in range(1, half):
+            q = (pair + i) % half
+            pltpu.make_async_copy(z_in.at[block, q], z_in.at[block, q], z_recv.at[block, q]).wait()
 
         @pl.loop(0, ny)
         def _(yy):
             total = [z_in[block, 0, yy, k] for k in range(4)]
-            for i in range(1, NZ):
+            for i in range(1, half):
                 total = over(total, [z_in[block, i, yy, k] for k in range(4)])
             for k in range(4):
                 y_part[block, yy, k] = total[k]
@@ -260,8 +296,10 @@
                 pltpu.make_async_copy(leave.at[block], leave.at[block], leave_send.at[d, block]).wait()
 
         core_copy(block).wait_send()
-        for d in range(1, NZ):
-            z_copy(block, d).wait_send()
+        for j in range(half):
+            pair_copy(block, j).wait_send()
+        for j in range(1, half):
+            z_copy(block, j).wait_send()
         for d in range(1, ny):
             y_copy(block, d).wait_send()
 
@@ -284,6 +322,8 @@
         scratch_shapes=[
             pltpu.VMEM((blocks, layers, slices // SUB, SUB * SUB, LANES), f32),
             pltpu.VMEM((blocks, slices, layers, SUB, LANES), f32),
+            pltpu.VMEM((blocks, slices, layers, SUB, LANES), jnp.int32),
+            pltpu.VMEM((blocks, slices, layers, SUB, LANES), f32),
             pltpu.VMEM((SUB, LANES), f32),
             pltpu.VMEM((blocks, layers * SUB, LANES), f32),
             pltpu.VMEM((nx, blocks, layers * SUB, LANES), f32),
@@ -291,7 +331,8 @@
             pltpu.VMEM((3, blocks, layers * SUB, LANES), f32),
             pltpu.VMEM((blocks, NCORE, NZ, ny, 4, SUB, LANES), f32),
             pltpu.VMEM((blocks, NZ, ny, 4, SUB, LANES), f32),
-            pltpu.VMEM((blocks, NZ, ny, 4, SUB, LANES), f32),
+            pltpu.VMEM((blocks, NZ // 2, ny, 4, SUB, LANES), f32),
+            pltpu.VMEM((blocks, NZ // 2, ny, 4, SUB, LANES), f32),
             pltpu.VMEM((blocks, ny, 4, SUB, LANES), f32),
             pltpu.VMEM((blocks, ny, 4, SUB, LANES), f32),
             pltpu.SemaphoreType.DMA((blocks,)),
@@ -299,8 +340,10 @@
             pltpu.SemaphoreType.DMA((nx, blocks)),
             pltpu.SemaphoreType.DMA((blocks,)),
             pltpu.SemaphoreType.DMA((blocks,)),
-            pltpu.SemaphoreType.DMA((blocks, NZ)),
-            pltpu.SemaphoreType.DMA((blocks, NZ)),
+            pltpu.SemaphoreType.DMA((blocks, NZ // 2)),
+            pltpu.SemaphoreType.DMA((blocks, NZ // 2)),
+            pltpu.SemaphoreType.DMA((blocks, NZ // 2)),
+            pltpu.SemaphoreType.DMA((blocks, NZ // 2)),
             pltpu.SemaphoreType.DMA((blocks, ny)),
             pltpu.SemaphoreType.DMA((blocks, ny)),
         ],

time: 91 us -> 80.7 us (0.89)
  Pallas kernels: 88.7 us -> 78.4 us
    pallas_call x1, Pallas kernels: 88.7 us -> 78.4 us  [local(): pl.pallas_call(functools.partial(kernel, nx, ny, layers, slices, columns,...]
where the time goes in v1:
time: 80.7 us; the launch traced here: 80.5 us
  Pallas kernels  78.4 us (97%)
  local copies, waits for them, and re-layouts  1.47 us (2%)
    pallas_call x1, Pallas kernels, local(): pl.pallas_call(functools.partial(kernel, nx, ny, layers, slices, columns,...  78.4 us

profile of v1, /device:TPU:6, one launch (start us, length us, event | category | flops | bytes accessed | tf_op | source)
XLA Modules:
  0.0 80.5 jit_solution(16477712840344848976)
XLA Ops:
  0.7 78.4 %shard_map.55 = f32[4,32,128]{2,1,0:T(8,128)} custom-call(s32[1,1]{1,0:T(1,128)S(6)} %copy.8.index_ref, s32[4]{0:T(128)} %code_ref.1, f32[4,3]{1,0:T(4,128)} %tint_ref.1, f32[8,4,16]{2,1,0:T(4,128)} %tables_ref.1, f32[8,8,256,128]{3,2,1,0:T(8,128)} %bitcast.6), custom_call_target="tpu_custom_call" | custom-call | tf_op jit(solution)/shard_map/pallas_call | solution.py:316
  79.1 1.5 %copy.9 = f32[4,1,4096]{2,1,0:T(1,128)} copy(f32[4,1,4096]{2,1,0:T(1,128)} %bitcast.7) | data formatting | bytes 131072

commit v2 on v1

--- a/solution.py
+++ b/solution.py
@@ -14,13 +14,13 @@
 NZ, NCORE = 8, 2
 
 
-def lookup(row, index):
+def take(table, index, axis):
     numbers = lax.GatherDimensionNumbers(
-        offset_dims=(), collapsed_slice_dims=(1,), start_index_map=(1,),
-        operand_batching_dims=(0,), start_indices_batching_dims=(0,),
+        offset_dims=(), collapsed_slice_dims=(axis,), start_index_map=(axis,),
+        operand_batching_dims=(1 - axis,), start_indices_batching_dims=(1 - axis,),
     )
     return lax.gather(
-        row, index[:, :, None], numbers, (1, 1), mode=lax.GatherScatterMode.PROMISE_IN_BOUNDS
+        table, index[:, :, None], numbers, (1, 1), mode=lax.GatherScatterMode.PROMISE_IN_BOUNDS
     )
 
 
@@ -67,17 +67,28 @@
     lane = lax.broadcasted_iota(jnp.int32, (SUB, LANES), 1)
     rise = jnp.where(lane < knots - 1, pltpu.roll(knot_values, LANES - 1, 1) - knot_values, 0.0)
     base = knot_values - rise * lane.astype(jnp.float32)
-    slope = rise * float(knots - 1)
     depth_scale = -math.log2(math.e) * math.exp2(-9)
-    rows = []
-    for q in range(4):
-        scale = depth_scale if q == 0 else 1.0
-        rows.append(
-            tuple(jnp.broadcast_to(t[q : q + 1] * scale, (SUB, LANES)) for t in (base, slope))
-        )
-
-    def cell_index(d):
-        return (d * float(knots - 1)).astype(jnp.int32)
+
+    def along_lanes(table, q):
+        return jnp.broadcast_to(table[q : q + 1], (SUB, LANES))
+
+    def along_sublanes(table, q):
+        sublane = lax.broadcasted_iota(jnp.int32, (SUB, LANES), 0)
+        halves = []
+        for first_knot in (0, SUB):
+            picked = jnp.where(lane == sublane + first_knot, along_lanes(table, q), 0.0)
+            halves.append(jnp.broadcast_to(jnp.sum(picked, axis=1, keepdims=True), (SUB, LANES)))
+        return halves
+
+    split = [(along_sublanes(base * s, q), along_sublanes(rise * s, q)) for q, s in ((0, depth_scale), (1, 1.0), (2, 1.0))]
+    whole = along_lanes(base, 3), along_lanes(rise, 3)
+
+    def level(q, scaled, k):
+        if q == 3:
+            return take(whole[0], k, 1) + take(whole[1], k, 1) * scaled
+        low = k & (SUB - 1)
+        parts = [jnp.where(scaled >= float(SUB), take(t[1], low, 0), take(t[0], low, 0)) for t in split[q]]
+        return parts[0] + parts[1] * scaled
 
     for block in range(blocks):
         pltpu.make_async_copy(dens.at[block], dens.at[block], dens_sem.at[block]).wait()
@@ -86,11 +97,11 @@
             sums = list(sums)
             for row in range(SUB):
                 for b in range(layers):
-                    d = dens[block, b, tile, pl.ds(row, SUB, stride=SUB), :]
-                    k = cell_index(d)
-                    depth = lookup(rows[0][0], k) + lookup(rows[0][1], k) * d
+                    scaled = dens[block, b, tile, pl.ds(row, SUB, stride=SUB), :] * float(knots - 1)
+                    k = scaled.astype(jnp.int32)
+                    depth = level(0, scaled, k)
                     keep[block, tile * SUB + row, b] = jnp.exp2(depth)
-                    cells[block, tile * SUB + row, b] = d
+                    cells[block, tile * SUB + row, b] = scaled
                     knot[block, tile * SUB + row, b] = k
                     sums[b] = sums[b] + depth
             return tuple(sums)
@@ -229,7 +240,7 @@
                 clear = None
                 total = [None] * 3
                 for b in range(layers):
-                    d = cells[block, tile * SUB + row, b]
+                    scaled = cells[block, tile * SUB + row, b]
                     k = knot[block, tile * SUB + row, b]
                     stays = keep[block, tile * SUB + row, b]
                     if clear is None:
@@ -241,7 +252,7 @@
                         clear = after
                     shadow[b] = shadow[b] * (stays * stays)
                     for c in range(3):
-                        color = lookup(rows[c + 1][0], k) + lookup(rows[c + 1][1], k) * d
+                        color = level(c + 1, scaled, k)
                         term = color * (weight * light[c, block, pl.ds(b * SUB, SUB), :])
                         total[c] = term if total[c] is None else total[c] + term
                 zz = (tile % 2) * (SUB // NCORE) + row // NCORE

time: 80.7 us -> 68.8 us (0.85)
  Pallas kernels: 78.4 us -> 66.4 us
    pallas_call x1, Pallas kernels: 78.4 us -> 66.4 us  [local(): pl.pallas_call(functools.partial(kernel, nx, ny, layers, slices, columns,...]
where the time goes in v2:
time: 68.8 us; the launch traced here: 68.6 us
  Pallas kernels  66.4 us (97%)
  local copies, waits for them, and re-layouts  1.47 us (2%)
    pallas_call x1, Pallas kernels, local(): pl.pallas_call(functools.partial(kernel, nx, ny, layers, slices, columns,...  66.4 us
    unnamed x1, local copies, waits for them, and re-layouts  1.47 us

profile of v2, /device:TPU:6, one launch (start us, length us, event | category | flops | bytes accessed | tf_op | source)
XLA Modules:
  0.0 68.6 jit_solution(5572884130782444316)
XLA Ops:
  0.7 66.4 %shard_map.55 = f32[4,32,128]{2,1,0:T(8,128)} custom-call(s32[1,1]{1,0:T(1,128)S(6)} %copy.8.index_ref, s32[4]{0:T(128)} %code_ref.1, f32[4,3]{1,0:T(4,128)} %tint_ref.1, f32[8,4,16]{2,1,0:T(4,128)} %tables_ref.1, f32[8,8,256,128]{3,2,1,0:T(8,128)} %bitcast.6), custom_call_target="tpu_custom_call" | custom-call | tf_op jit(solution)/shard_map/pallas_call | solution.py:327
  67.1 1.5 %copy.9 = f32[4,1,4096]{2,1,0:T(1,128)} copy(f32[4,1,4096]{2,1,0:T(1,128)} %bitcast.7) | data formatting | bytes 131072

commit v3 on v2

--- a/solution.py
+++ b/solution.py
@@ -32,8 +32,10 @@
 def kernel(
     nx, ny, layers, slices, columns, knots, table_count, lights,
     index_ref, code_ref, tint_ref, tables_ref, density_ref, out_ref,
-    dens, cells, knot, keep, tab, leave, leave_in, fronts, light, part, core_in, pair_in, z_in, y_part, y_in,
-    dens_sem, leave_send, leave_recv, core_send, core_recv, pair_send, pair_recv, z_send, z_recv, y_send, y_recv,
+    dens, cells, knot, keep, tab, leave, leave_in, fronts, light, shades,
+    part, core_in, up_in, down_in, cross_in, y_part, y_in, rest, rest_in,
+    dens_sem, leave_send, leave_recv, core_send, core_recv, up_send, up_recv, down_send, down_recv,
+    cross_send, cross_recv, y_send, y_recv, rest_send, rest_recv,
 ):
     x = lax.axis_index("light")
     v = lax.axis_index("view")
@@ -54,7 +56,7 @@
 
     barrier = pltpu.get_barrier_semaphore()
     peers = [at_view(y, z, 1 - core)]
-    peers += [at_view(y, (z + d) % NZ, core) for d in range(1, NZ)]
+    peers += [at_view(y, (z + d) % NZ, core) for d in (1, NZ - 1)]
     peers += [at_view((y + d) % ny, z, core) for d in range(1, ny)]
     peers += [{"light": (x + d) % nx} for d in range(1, nx)]
     for peer in peers:
@@ -159,83 +161,76 @@
                 fronts[0, :, cols] * tint[0] + fronts[1, :, cols] * tint[1] + fronts[2, :, cols] * tint[2]
             )
 
-    def core_copy(block):
-        return pltpu.make_async_remote_copy(
-            src_ref=part.at[block, 1 - core], dst_ref=core_in.at[block],
-            send_sem=core_send.at[block], recv_sem=core_recv.at[block],
+    pieces = blocks * ny
+    quad = NZ // 2
+    half = z // quad
+    q = z % quad
+    last = quad - 1
+    up_base = half * quad
+    down_base = quad - up_base
+    own_base = (z + NZ - 2 - q // last) % NZ
+    toward = 2 * (q // last) - 1
+    own = q // last
+
+    def core_copy(n):
+        return pltpu.make_async_remote_copy(
+            src_ref=part.at[n, 1 - core], dst_ref=core_in.at[n],
+            send_sem=core_send.at[n], recv_sem=core_recv.at[n],
             device_id=at_view(y, z, 1 - core), device_id_type=MESH,
         )
 
-    pair = z // 2
-    odd = z % 2
-    side = 2 * odd - 1
-    half = NZ // 2
-
-    def owner(j):
-        return (z + side * j + NZ) % NZ
-
-    def pair_copy(block, j):
-        return pltpu.make_async_remote_copy(
-            src_ref=part.at[block, core, owner(-1 - j)], dst_ref=pair_in.at[block, j],
-            send_sem=pair_send.at[block, j], recv_sem=pair_recv.at[block, j],
-            device_id=at_view(y, owner(-1), core), device_id_type=MESH,
-        )
-
-    def z_copy(block, j):
-        return pltpu.make_async_remote_copy(
-            src_ref=part.at[block, core, owner(j)], dst_ref=z_in.at[block, pair],
-            send_sem=z_send.at[block, j], recv_sem=z_recv.at[block, pair],
-            device_id=at_view(y, owner(j), core), device_id_type=MESH,
-        )
-
-    def y_copy(block, d):
-        to = (y + d) % ny
-        return pltpu.make_async_remote_copy(
-            src_ref=y_part.at[block, to], dst_ref=y_in.at[block, y],
-            send_sem=y_send.at[block, d], recv_sem=y_recv.at[block, y],
+    def up_copy(n):
+        return pltpu.make_async_remote_copy(
+            src_ref=part.at[n, core, pl.ds(up_base, quad)], dst_ref=up_in.at[n],
+            send_sem=up_send.at[n], recv_sem=up_recv.at[n],
+            device_id=at_view(y, (z + 1) % NZ, core), device_id_type=MESH,
+        )
+
+    def down_copy(n):
+        return pltpu.make_async_remote_copy(
+            src_ref=part.at[n, core, pl.ds(down_base, quad)], dst_ref=down_in.at[n],
+            send_sem=down_send.at[n], recv_sem=down_recv.at[n],
+            device_id=at_view(y, (z + NZ - 1) % NZ, core), device_id_type=MESH,
+        )
+
+    def cross_copy(n):
+        return pltpu.make_async_remote_copy(
+            src_ref=part.at[n, core, pl.ds((own_base + 2 * toward + NZ) % NZ, 2)], dst_ref=cross_in.at[n],
+            send_sem=cross_send.at[n], recv_sem=cross_recv.at[n],
+            device_id=at_view(y, (z + toward + NZ) % NZ, core), device_id_type=MESH,
+        )
+
+    def y_copy(n, to, source):
+        return pltpu.make_async_remote_copy(
+            src_ref=y_part.at[n], dst_ref=y_in.at[n // ny, source],
+            send_sem=y_send.at[n], recv_sem=y_recv.at[n // ny, source],
             device_id=at_view(to, z, core), device_id_type=MESH,
         )
+
+    def rest_copy(block):
+        return pltpu.make_async_remote_copy(
+            src_ref=rest.at[block], dst_ref=rest_in.at[block],
+            send_sem=rest_send.at[block], recv_sem=rest_recv.at[block],
+            device_id=at_view(y, (z - toward + NZ) % NZ, core), device_id_type=MESH,
+        )
+
+    is_end = jnp.logical_or(q == 0, q == last)
 
     def ordered(later, mine, other):
         front = [jnp.where(later, o, m) for m, o in zip(mine, other)]
         back = [jnp.where(later, m, o) for m, o in zip(mine, other)]
         return over(front, back)
 
-    def join_cores(block):
-        core_copy(block).wait_recv()
-
-        @pl.loop(0, NZ)
-        def _(zz):
-            for yy in range(ny):
-                mine = [part[block, core, zz, yy, k] for k in range(4)]
-                other = [core_in[block, zz, yy, k] for k in range(4)]
-                joined = ordered(core == 1, mine, other)
-                for k in range(4):
-                    part[block, core, zz, yy, k] = joined[k]
-
-        for j in reversed(range(half)):
-            pair_copy(block, j).start()
-
-    def join_pair(block):
-        for j in reversed(range(half)):
-            pair_copy(block, j).wait_recv()
-            at = owner(j)
-            for yy in range(ny):
-                mine = [part[block, core, at, yy, k] for k in range(4)]
-                other = [pair_in[block, j, yy, k] for k in range(4)]
-                joined = ordered(odd == 1, mine, other)
-                for k in range(4):
-                    if j:
-                        part[block, core, at, yy, k] = joined[k]
-                    else:
-                        z_in[block, pair, yy, k] = joined[k]
-            if j:
-                z_copy(block, j).start()
-
-    for block in range(blocks):
-
-        def second(tile, shadow, block=block):
+    def second(n):
+        block, yy = n // ny, n % ny
+
+        @pl.when(yy == 0)
+        def _():
+            shades[...] = jnp.ones_like(shades)
+
+        def rows(i, shadow):
             shadow = list(shadow)
+            tile = yy * 2 + i
             for row in range(SUB):
                 clear = None
                 total = [None] * 3
@@ -255,49 +250,131 @@
                         color = level(c + 1, scaled, k)
                         term = color * (weight * light[c, block, pl.ds(b * SUB, SUB), :])
                         total[c] = term if total[c] is None else total[c] + term
-                zz = (tile % 2) * (SUB // NCORE) + row // NCORE
+                slot = (i * (SUB // NCORE) + row // NCORE + NZ - 2) % NZ
                 for c in range(3):
-                    part[block, row % NCORE, zz, tile // 2, c] = total[c]
-                part[block, row % NCORE, zz, tile // 2, 3] = clear
+                    part[n, row % NCORE, slot, c] = total[c]
+                part[n, row % NCORE, slot, 3] = clear
             return tuple(shadow)
 
-        one = jnp.ones((SUB, LANES), jnp.float32)
-        lax.fori_loop(0, tiles_a, second, (one,) * layers)
-        core_copy(block).start()
-        if block:
-            join_cores(block - 1)
-    join_cores(blocks - 1)
-
-    for block in range(blocks):
-        join_pair(block)
-
-    for block in range(blocks):
-        for i in range(1, half):
-            q = (pair + i) % half
-            pltpu.make_async_copy(z_in.at[block, q], z_in.at[block, q], z_recv.at[block, q]).wait()
-
-        @pl.loop(0, ny)
-        def _(yy):
-            total = [z_in[block, 0, yy, k] for k in range(4)]
-            for i in range(1, half):
-                total = over(total, [z_in[block, i, yy, k] for k in range(4)])
+        shadow = lax.fori_loop(0, 2, rows, tuple(shades[b] for b in range(layers)))
+        for b in range(layers):
+            shades[b] = shadow[b]
+
+    def join(n, first, count, incoming, later):
+        for i in range(count):
+            mine = [part[n, core, first + i, k] for k in range(4)]
+            joined = ordered(later, mine, [incoming[n, i, k] for k in range(4)])
             for k in range(4):
-                y_part[block, yy, k] = total[k]
-
-        for d in range(1, ny):
-            y_copy(block, d).start()
-        for k in range(4):
-            y_in[block, y, k] = y_part[block, y, k]
-
-    for block in range(blocks):
-        for i in range(1, ny):
-            yy = (y + i) % ny
-            pltpu.make_async_copy(y_in.at[block, yy], y_in.at[block, yy], y_recv.at[block, yy]).wait()
-        total = [y_in[block, 0, k] for k in range(4)]
-        for i in range(1, ny):
-            total = over(total, [y_in[block, i, k] for k in range(4)])
-        for k in range(4):
-            out_ref[k, pl.ds(block * SUB, SUB)] = total[k]
+                part[n, core, first + i, k] = joined[k]
+
+    def due(n):
+        return jnp.logical_and(n >= 0, n < pieces)
+
+    core_lag, hop_lag, y_lag = 2, 3, 2
+    steps = pieces + core_lag + last * hop_lag + hop_lag + y_lag
+
+    @pl.loop(0, steps)
+    def _(step):
+        @pl.when(step < pieces)
+        def _():
+            second(step)
+            core_copy(step).start()
+
+        at = step - core_lag
+
+        @pl.when(due(at))
+        def _():
+            core_copy(at).wait_recv()
+            join(at, 0, NZ, core_in, core == 1)
+
+            @pl.when(q == 0)
+            def _():
+                up_copy(at).start()
+
+            @pl.when(q == last)
+            def _():
+                down_copy(at).start()
+
+        up_at = at - hop_lag * q
+
+        @pl.when(jnp.logical_and(due(up_at), q > 0))
+        def _():
+            up_copy(up_at).wait_recv()
+            join(up_at, up_base, quad, up_in, q > 0)
+
+            @pl.when(q < last)
+            def _():
+                up_copy(up_at).start()
+
+            @pl.when(q == last)
+            def _():
+                cross_copy(up_at).start()
+
+        down_at = at - hop_lag * (last - q)
+
+        @pl.when(jnp.logical_and(due(down_at), q < last))
+        def _():
+            down_copy(down_at).wait_recv()
+            join(down_at, down_base, quad, down_in, q < 0)
+
+            @pl.when(q > 0)
+            def _():
+                down_copy(down_at).start()
+
+            @pl.when(q == 0)
+            def _():
+                cross_copy(down_at).start()
+
+        cross_at = at - hop_lag * last - hop_lag
+
+        @pl.when(jnp.logical_and(due(cross_at), is_end))
+        def _():
+            cross_copy(cross_at).wait_recv()
+            to = cross_at % ny
+            for i in range(2):
+                mine = [part[cross_at, core, own_base + i, k] for k in range(4)]
+                joined = ordered(half == 1, mine, [cross_in[cross_at, i, k] for k in range(4)])
+                for k in range(4):
+                    y_part[cross_at, i, k] = joined[k]
+
+            @pl.when(to != y)
+            def _():
+                y_copy(cross_at, to, y).start()
+
+        y_at = cross_at - y_lag
+
+        @pl.when(jnp.logical_and(jnp.logical_and(due(y_at), is_end), y_at % ny == y))
+        def _():
+            block = y_at // ny
+            for i in range(1, ny):
+                source = (y + i) % ny
+                y_copy(y_at, source, source).wait_recv()
+            for i in range(2):
+                for k in range(4):
+                    y_in[block, y, i, k] = y_part[y_at, i, k]
+            for i in range(2):
+                total = [y_in[block, 0, i, k] for k in range(4)]
+                for j in range(1, ny):
+                    total = over(total, [y_in[block, j, i, k] for k in range(4)])
+
+                @pl.when(own == i)
+                def _():
+                    for k in range(4):
+                        out_ref[k, pl.ds(block * SUB, SUB)] = total[k]
+
+                @pl.when(own != i)
+                def _():
+                    for k in range(4):
+                        rest[block, k] = total[k]
+
+            rest_copy(block).start()
+
+    @pl.when(jnp.logical_not(is_end))
+    def _():
+        for block in range(blocks):
+            rest_copy(block).wait_recv()
+            for k in range(4):
+                out_ref[k, pl.ds(block * SUB, SUB)] = rest_in[block, k]
 
     for block in range(blocks):
         for d in range(1, nx):
@@ -306,13 +383,30 @@
             def _(d=d, block=block):
                 pltpu.make_async_copy(leave.at[block], leave.at[block], leave_send.at[d, block]).wait()
 
-        core_copy(block).wait_send()
-        for j in range(half):
-            pair_copy(block, j).wait_send()
-        for j in range(1, half):
-            z_copy(block, j).wait_send()
-        for d in range(1, ny):
-            y_copy(block, d).wait_send()
+    @pl.loop(0, pieces)
+    def _(n):
+        core_copy(n).wait_send()
+
+        @pl.when(q < last)
+        def _():
+            up_copy(n).wait_send()
+
+        @pl.when(q > 0)
+        def _():
+            down_copy(n).wait_send()
+
+        @pl.when(is_end)
+        def _():
+            cross_copy(n).wait_send()
+
+            @pl.when(n % ny != y)
+            def _():
+                y_copy(n, n % ny, y).wait_send()
+
+    @pl.when(is_end)
+    def _():
+        for block in range(blocks):
+            rest_copy(block).wait_send()
 
 
 def local(density, tables, table_index, light_code, light_tint):
@@ -323,6 +417,7 @@
     blocks = tiles // SUB
     tiled = density.reshape(layers, slices // SUB, SUB, tiles, LANES).transpose(0, 1, 3, 2, 4)
     tiled = tiled.reshape(layers, slices // SUB, tiles * SUB, LANES)
+    pieces = blocks * ny
     f32 = jnp.float32
     image = pl.pallas_call(
         functools.partial(kernel, nx, ny, layers, slices, columns, knots, table_count, light_code.shape[0]),
@@ -340,23 +435,25 @@
             pltpu.VMEM((nx, blocks, layers * SUB, LANES), f32),
             pltpu.VMEM((3, layers, columns), f32),
             pltpu.VMEM((3, blocks, layers * SUB, LANES), f32),
-            pltpu.VMEM((blocks, NCORE, NZ, ny, 4, SUB, LANES), f32),
-            pltpu.VMEM((blocks, NZ, ny, 4, SUB, LANES), f32),
-            pltpu.VMEM((blocks, NZ // 2, ny, 4, SUB, LANES), f32),
-            pltpu.VMEM((blocks, NZ // 2, ny, 4, SUB, LANES), f32),
-            pltpu.VMEM((blocks, ny, 4, SUB, LANES), f32),
-            pltpu.VMEM((blocks, ny, 4, SUB, LANES), f32),
+            pltpu.VMEM((layers, SUB, LANES), f32),
+            pltpu.VMEM((pieces, NCORE, NZ, 4, SUB, LANES), f32),
+            pltpu.VMEM((pieces, NZ, 4, SUB, LANES), f32),
+            pltpu.VMEM((pieces, NZ // 2, 4, SUB, LANES), f32),
+            pltpu.VMEM((pieces, NZ // 2, 4, SUB, LANES), f32),
+            pltpu.VMEM((pieces, 2, 4, SUB, LANES), f32),
+            pltpu.VMEM((pieces, 2, 4, SUB, LANES), f32),
+            pltpu.VMEM((blocks, ny, 2, 4, SUB, LANES), f32),
+            pltpu.VMEM((blocks, 4, SUB, LANES), f32),
+            pltpu.VMEM((blocks, 4, SUB, LANES), f32),
             pltpu.SemaphoreType.DMA((blocks,)),
             pltpu.SemaphoreType.DMA((nx, blocks)),
             pltpu.SemaphoreType.DMA((nx, blocks)),
+        ]
+        + [pltpu.SemaphoreType.DMA((pieces,))] * 9
+        + [
+            pltpu.SemaphoreType.DMA((blocks, ny)),
             pltpu.SemaphoreType.DMA((blocks,)),
             pltpu.SemaphoreType.DMA((blocks,)),
-            pltpu.SemaphoreType.DMA((blocks, NZ // 2)),
-            pltpu.SemaphoreType.DMA((blocks, NZ // 2)),
-            pltpu.SemaphoreType.DMA((blocks, NZ // 2)),
-            pltpu.SemaphoreType.DMA((blocks, NZ // 2)),
-            pltpu.SemaphoreType.DMA((blocks, ny)),
-            pltpu.SemaphoreType.DMA((blocks, ny)),
         ],
         compiler_params=pltpu.CompilerParams(
             collective_id=0, has_side_effects=True, vmem_limit_bytes=60 * 1024 * 1024

time: 68.8 us -> 65.2 us (0.948)
  the two profiles are of different devices: /device:TPU:6 before, /device:TPU:62 now
where the time goes in v3:
time: 65.2 us; the launch traced here: 65.1 us
  Pallas kernels  62.9 us (96%)
  local copies, waits for them, and re-layouts  1.47 us (2%)
  between operations  0.66 us (1%)
    pallas_call x1, Pallas kernels, local(): pl.pallas_call(functools.partial(kernel, nx, ny, layers, slices, columns,...  62.9 us
    unnamed x1, local copies, waits for them, and re-layouts  1.47 us

profile of v3, /device:TPU:62, one launch (start us, length us, event | category | flops | bytes accessed | tf_op | source)
XLA Modules:
  0.0 65.1 jit_solution(9758477839378595191)
XLA Ops:
  0.7 62.9 %shard_map.55 = f32[4,32,128]{2,1,0:T(8,128)} custom-call(s32[1,1]{1,0:T(1,128)S(6)} %copy.8.index_ref, s32[4]{0:T(128)} %code_ref.1, f32[4,3]{1,0:T(4,128)} %tint_ref.1, f32[8,4,16]{2,1,0:T(4,128)} %tables_ref.1, f32[8,8,256,128]{3,2,1,0:T(8,128)} %bitcast.6), custom_call_target="tpu_custom_call" | custom-call | tf_op jit(solution)/shard_map/pallas_call | solution.py:422
  63.6 1.5 %copy.9 = f32[4,1,4096]{2,1,0:T(1,128)} copy(f32[4,1,4096]{2,1,0:T(1,128)} %bitcast.7) | data formatting | bytes 131072

commit v4 on v3

--- a/solution.py
+++ b/solution.py
@@ -92,10 +92,17 @@
         parts = [jnp.where(scaled >= float(SUB), take(t[1], low, 0), take(t[0], low, 0)) for t in split[q]]
         return parts[0] + parts[1] * scaled
 
-    for block in range(blocks):
+    def leave_copy(block, d):
+        return pltpu.make_async_remote_copy(
+            src_ref=leave.at[block], dst_ref=leave_in.at[x, block],
+            send_sem=leave_send.at[d, block], recv_sem=leave_recv.at[x, block],
+            device_id={"light": (x + d) % nx}, device_id_type=MESH,
+        )
+
+    def first(block):
         pltpu.make_async_copy(dens.at[block], dens.at[block], dens_sem.at[block]).wait()
 
-        def first(tile, sums, block=block):
+        def rows(tile, sums):
             sums = list(sums)
             for row in range(SUB):
                 for b in range(layers):
@@ -109,7 +116,7 @@
             return tuple(sums)
 
         zero = jnp.zeros((SUB, LANES), jnp.float32)
-        sums = lax.fori_loop(0, tiles_a, first, (zero,) * layers)
+        sums = lax.fori_loop(0, tiles_a, rows, (zero,) * layers)
         for b in range(layers):
             leave[block, pl.ds(b * SUB, SUB)] = jnp.exp2(sums[b] * 2.0)
         if block == 0:
@@ -117,49 +124,52 @@
         for d in range(1, nx):
 
             @pl.when(x + d < nx)
-            def _(d=d, block=block):
-                pltpu.make_async_remote_copy(
-                    src_ref=leave.at[block], dst_ref=leave_in.at[x, block],
-                    send_sem=leave_send.at[d, block], recv_sem=leave_recv.at[x, block],
-                    device_id={"light": (x + d) % nx}, device_id_type=MESH,
-                ).start()
-
-    column = lax.broadcasted_iota(jnp.int32, (layers, columns), 1)
-    fronts[...] = jnp.ones_like(fronts)
-
-    def moved(values, by):
-        rolled = pltpu.roll(values, by % columns, 1)
-        inside = column >= by if by > 0 else column < columns + by
-        return jnp.where(inside, rolled, 0.0)
-
-    for stage in range(nx - 1):
-
-        @pl.when(x > stage)
-        def _(stage=stage):
-            for block in range(blocks):
+            def _(d=d):
+                leave_copy(block, d).start()
+
+    wide = (SUB + 2) * LANES
+
+    def light_up(block):
+        fronts[...] = jnp.ones_like(fronts)
+        before = jnp.maximum(block - 1, 0)
+        behind = jnp.minimum(block + 1, blocks - 1)
+        for stage in range(nx - 1):
+
+            @pl.when(x > stage)
+            def _(stage=stage):
+                def gone_of(at, t):
+                    return leave_in[stage, at, pl.ds(t, layers, stride=SUB), :]
+
+                gone = [jnp.where(block > 0, gone_of(before, SUB - 1), 0.0)]
+                gone += [gone_of(block, t) for t in range(SUB)]
+                gone += [jnp.where(block < blocks - 1, gone_of(behind, 0), 0.0)]
+                gone = jnp.concatenate(gone, axis=1)
+                for drift in (-1, 0, 1):
+                    value = fronts[drift + 1] * gone
+                    sides = pltpu.roll(value, (drift - 1) % wide, 1) if drift != 1 else value
+                    sides = sides + (pltpu.roll(value, (drift + 1) % wide, 1) if drift != -1 else value)
+                    center = pltpu.roll(value, drift % wide, 1) if drift else value
+                    fronts[drift + 1] = 0.25 * sides + 0.5 * center
+
+        for k in range(3):
+            tint = [0.0, 0.0, 0.0]
+            for l in range(lights):
+                for drift in (-1, 0, 1):
+                    tint[drift + 1] = tint[drift + 1] + jnp.where(code_ref[l] == drift, tint_ref[l, k], 0.0)
+            for t in range(SUB):
+                cols = pl.ds((t + 1) * LANES, LANES)
+                light[k, block, pl.ds(t, layers, stride=SUB), :] = (
+                    fronts[0, :, cols] * tint[0] + fronts[1, :, cols] * tint[1] + fronts[2, :, cols] * tint[2]
+                )
+
+    def leaves_arrive(block):
+        for stage in range(nx - 1):
+
+            @pl.when(x > stage)
+            def _(stage=stage):
                 pltpu.make_async_copy(
                     leave_in.at[stage, block], leave_in.at[stage, block], leave_recv.at[stage, block]
                 ).wait()
-            gone = jnp.concatenate(
-                [leave_in[stage, t // SUB, pl.ds(t % SUB, layers, stride=SUB), :] for t in range(tiles)], axis=1
-            )
-            for drift in (-1, 0, 1):
-                value = fronts[drift + 1] * gone
-                total = 0.0
-                for offset, share in ((drift - 1, 0.25), (drift, 0.5), (drift + 1, 0.25)):
-                    total = total + share * (moved(value, offset) if offset else value)
-                fronts[drift + 1] = total
-
-    for k in range(3):
-        tint = [0.0, 0.0, 0.0]
-        for l in range(lights):
-            for drift in (-1, 0, 1):
-                tint[drift + 1] = tint[drift + 1] + jnp.where(code_ref[l] == drift, tint_ref[l, k], 0.0)
-        for t in range(tiles):
-            cols = pl.ds(t * LANES, LANES)
-            light[k, t // SUB, pl.ds(t % SUB, layers, stride=SUB), :] = (
-                fronts[0, :, cols] * tint[0] + fronts[1, :, cols] * tint[1] + fronts[2, :, cols] * tint[2]
-            )
 
     pieces = blocks * ny
     quad = NZ // 2
@@ -270,11 +280,34 @@
     def due(n):
         return jnp.logical_and(n >= 0, n < pieces)
 
-    core_lag, hop_lag, y_lag = 2, 3, 2
-    steps = pieces + core_lag + last * hop_lag + hop_lag + y_lag
+    core_lag, hop_lag, cross_lag, y_lag = 1, 3, 6, 6
+    steps = pieces + core_lag + last * hop_lag + cross_lag + y_lag
+
+    ahead = blocks - 1
+    for block in range(ahead):
+        first(block)
 
     @pl.loop(0, steps)
     def _(step):
+        @pl.when(step == 1)
+        def _():
+            for block in range(ahead, blocks):
+                first(block)
+
+        @pl.when(jnp.logical_and(step % ny == 0, step < pieces))
+        def _():
+            block = step // ny
+
+            @pl.when(block == 0)
+            def _():
+                leaves_arrive(0)
+
+            @pl.when(block < blocks - 1)
+            def _():
+                leaves_arrive(block + 1)
+
+            light_up(block)
+
         @pl.when(step < pieces)
         def _():
             second(step)
@@ -325,7 +358,7 @@
             def _():
                 cross_copy(down_at).start()
 
-        cross_at = at - hop_lag * last - hop_lag
+        cross_at = at - hop_lag * last - cross_lag
 
         @pl.when(jnp.logical_and(due(cross_at), is_end))
         def _():
@@ -381,7 +414,7 @@
 
             @pl.when(x + d < nx)
             def _(d=d, block=block):
-                pltpu.make_async_copy(leave.at[block], leave.at[block], leave_send.at[d, block]).wait()
+                leave_copy(block, d).wait_send()
 
     @pl.loop(0, pieces)
     def _(n):
@@ -433,7 +466,7 @@
             pltpu.VMEM((SUB, LANES), f32),
             pltpu.VMEM((blocks, layers * SUB, LANES), f32),
             pltpu.VMEM((nx, blocks, layers * SUB, LANES), f32),
-            pltpu.VMEM((3, layers, columns), f32),
+            pltpu.VMEM((3, layers, (SUB + 2) * LANES), f32),
             pltpu.VMEM((3, blocks, layers * SUB, LANES), f32),
             pltpu.VMEM((layers, SUB, LANES), f32),
             pltpu.VMEM((pieces, NCORE, NZ, 4, SUB, LANES), f32),

time: 65.2 us -> 62.2 us (0.954)
  Pallas kernels: 62.9 us -> 59.8 us
    pallas_call x1, Pallas kernels: 62.9 us -> 59.8 us  [local(): pl.pallas_call(functools.partial(kernel, nx, ny, layers, slices, columns,...]
where the time goes in v4:
time: 62.2 us; the launch traced here: 62 us
  Pallas kernels  59.8 us (96%)
  local copies, waits for them, and re-layouts  1.47 us (2%)
  between operations  0.66 us (1%)
    pallas_call x1, Pallas kernels, local(): pl.pallas_call(functools.partial(kernel, nx, ny, layers, slices, columns,...  59.8 us
    unnamed x1, local copies, waits for them, and re-layouts  1.47 us

profile of v4, /device:TPU:62, one launch (start us, length us, event | category | flops | bytes accessed | tf_op | source)
XLA Modules:
  0.0 62.0 jit_solution(766959833367910560)
XLA Ops:
  0.7 59.8 %shard_map.55 = f32[4,32,128]{2,1,0:T(8,128)} custom-call(s32[1,1]{1,0:T(1,128)S(6)} %copy.8.index_ref, s32[4]{0:T(128)} %code_ref.1, f32[4,3]{1,0:T(4,128)} %tint_ref.1, f32[8,4,16]{2,1,0:T(4,128)} %tables_ref.1, f32[8,8,256,128]{3,2,1,0:T(8,128)} %bitcast.6), custom_call_target="tpu_custom_call" | custom-call | tf_op jit(solution)/shard_map/pallas_call | solution.py:455
  60.5 1.5 %copy.9 = f32[4,1,4096]{2,1,0:T(1,128)} copy(f32[4,1,4096]{2,1,0:T(1,128)} %bitcast.7) | data formatting | bytes 131072

commit v5 on v4

--- a/solution.py
+++ b/solution.py
@@ -33,9 +33,9 @@
     nx, ny, layers, slices, columns, knots, table_count, lights,
     index_ref, code_ref, tint_ref, tables_ref, density_ref, out_ref,
     dens, cells, knot, keep, tab, leave, leave_in, fronts, light, shades,
-    part, core_in, up_in, down_in, cross_in, y_part, y_in, rest, rest_in,
+    part, core_in, up_in, down_in, cross_in, y_part, y_in,
     dens_sem, leave_send, leave_recv, core_send, core_recv, up_send, up_recv, down_send, down_recv,
-    cross_send, cross_recv, y_send, y_recv, rest_send, rest_recv,
+    cross_send, cross_recv, y_send, y_recv, rest_send,
 ):
     x = lax.axis_index("light")
     v = lax.axis_index("view")
@@ -58,6 +58,7 @@
     peers = [at_view(y, z, 1 - core)]
     peers += [at_view(y, (z + d) % NZ, core) for d in (1, NZ - 1)]
     peers += [at_view((y + d) % ny, z, core) for d in range(1, ny)]
+    peers += [at_view((y + d) % ny, z + 1 - 2 * (z % 2), core) for d in range(1, ny)]
     peers += [{"light": (x + d) % nx} for d in range(1, nx)]
     for peer in peers:
         pl.semaphore_signal(barrier, inc=1, device_id=peer, device_id_type=MESH)
@@ -210,18 +211,20 @@
             device_id=at_view(y, (z + toward + NZ) % NZ, core), device_id_type=MESH,
         )
 
+    buddy = z + 1 - 2 * (z % 2)
+
     def y_copy(n, to, source):
         return pltpu.make_async_remote_copy(
-            src_ref=y_part.at[n], dst_ref=y_in.at[n // ny, source],
+            src_ref=y_part.at[n, own], dst_ref=y_in.at[n // ny, source],
             send_sem=y_send.at[n], recv_sem=y_recv.at[n // ny, source],
             device_id=at_view(to, z, core), device_id_type=MESH,
         )
 
-    def rest_copy(block):
-        return pltpu.make_async_remote_copy(
-            src_ref=rest.at[block], dst_ref=rest_in.at[block],
-            send_sem=rest_send.at[block], recv_sem=rest_recv.at[block],
-            device_id=at_view(y, (z - toward + NZ) % NZ, core), device_id_type=MESH,
+    def buddy_copy(n, to, source):
+        return pltpu.make_async_remote_copy(
+            src_ref=y_part.at[n, 1 - own], dst_ref=y_in.at[n // ny, source],
+            send_sem=rest_send.at[n], recv_sem=y_recv.at[n // ny, source],
+            device_id=at_view(to, buddy, core), device_id_type=MESH,
         )
 
     is_end = jnp.logical_or(q == 0, q == last)
@@ -374,40 +377,31 @@
             def _():
                 y_copy(cross_at, to, y).start()
 
+            buddy_copy(cross_at, to, y).start()
+
         y_at = cross_at - y_lag
 
-        @pl.when(jnp.logical_and(jnp.logical_and(due(y_at), is_end), y_at % ny == y))
+        @pl.when(jnp.logical_and(due(y_at), y_at % ny == y))
         def _():
             block = y_at // ny
+
+            @pl.when(is_end)
+            def _():
+                for k in range(4):
+                    y_in[block, y, k] = y_part[y_at, own, k]
+
+            @pl.when(jnp.logical_not(is_end))
+            def _():
+                y_copy(y_at, y, y).wait_recv()
+
             for i in range(1, ny):
                 source = (y + i) % ny
                 y_copy(y_at, source, source).wait_recv()
-            for i in range(2):
-                for k in range(4):
-                    y_in[block, y, i, k] = y_part[y_at, i, k]
-            for i in range(2):
-                total = [y_in[block, 0, i, k] for k in range(4)]
-                for j in range(1, ny):
-                    total = over(total, [y_in[block, j, i, k] for k in range(4)])
-
-                @pl.when(own == i)
-                def _():
-                    for k in range(4):
-                        out_ref[k, pl.ds(block * SUB, SUB)] = total[k]
-
-                @pl.when(own != i)
-                def _():
-                    for k in range(4):
-                        rest[block, k] = total[k]
-
-            rest_copy(block).start()
-
-    @pl.when(jnp.logical_not(is_end))
-    def _():
-        for block in range(blocks):
-            rest_copy(block).wait_recv()
+            total = [y_in[block, 0, k] for k in range(4)]
+            for j in range(1, ny):
+                total = over(total, [y_in[block, j, k] for k in range(4)])
             for k in range(4):
-                out_ref[k, pl.ds(block * SUB, SUB)] = rest_in[block, k]
+                out_ref[k, pl.ds(block * SUB, SUB)] = total[k]
 
     for block in range(blocks):
         for d in range(1, nx):
@@ -431,15 +425,11 @@
         @pl.when(is_end)
         def _():
             cross_copy(n).wait_send()
+            buddy_copy(n, n % ny, y).wait_send()
 
             @pl.when(n % ny != y)
             def _():
                 y_copy(n, n % ny, y).wait_send()
-
-    @pl.when(is_end)
-    def _():
-        for block in range(blocks):
-            rest_copy(block).wait_send()
 
 
 def local(density, tables, table_index, light_code, light_tint):
@@ -475,9 +465,7 @@
             pltpu.VMEM((pieces, NZ // 2, 4, SUB, LANES), f32),
             pltpu.VMEM((pieces, 2, 4, SUB, LANES), f32),
             pltpu.VMEM((pieces, 2, 4, SUB, LANES), f32),
-            pltpu.VMEM((blocks, ny, 2, 4, SUB, LANES), f32),
-            pltpu.VMEM((blocks, 4, SUB, LANES), f32),
-            pltpu.VMEM((blocks, 4, SUB, LANES), f32),
+            pltpu.VMEM((blocks, ny, 4, SUB, LANES), f32),
             pltpu.SemaphoreType.DMA((blocks,)),
             pltpu.SemaphoreType.DMA((nx, blocks)),
             pltpu.SemaphoreType.DMA((nx, blocks)),
@@ -485,8 +473,7 @@
         + [pltpu.SemaphoreType.DMA((pieces,))] * 9
         + [
             pltpu.SemaphoreType.DMA((blocks, ny)),
-            pltpu.SemaphoreType.DMA((blocks,)),
-            pltpu.SemaphoreType.DMA((blocks,)),
+            pltpu.SemaphoreType.DMA((pieces,)),
         ],
         compiler_params=pltpu.CompilerParams(
             collective_id=0, has_side_effects=True, vmem_limit_bytes=60 * 1024 * 1024

time: 62.2 us -> 60.3 us (0.969)
  the two profiles are of different devices: /device:TPU:62 before, /device:TPU:30 now
where the time goes in v5:
time: 60.3 us; the launch traced here: 60.1 us
  Pallas kernels  57.9 us (96%)
  local copies, waits for them, and re-layouts  1.47 us (2%)
  between operations  0.66 us (1%)
    pallas_call x1, Pallas kernels, local(): pl.pallas_call(functools.partial(kernel, nx, ny, layers, slices, columns,...  57.9 us
    unnamed x1, local copies, waits for them, and re-layouts  1.47 us

profile of v5, /device:TPU:30, one launch (start us, length us, event | category | flops | bytes accessed | tf_op | source)
XLA Modules:
  0.0 60.1 jit_solution(14631329953725671199)
XLA Ops:
  0.7 57.9 %shard_map.55 = f32[4,32,128]{2,1,0:T(8,128)} custom-call(s32[1,1]{1,0:T(1,128)S(6)} %copy.8.index_ref, s32[4]{0:T(128)} %code_ref.1, f32[4,3]{1,0:T(4,128)} %tint_ref.1, f32[8,4,16]{2,1,0:T(4,128)} %tables_ref.1, f32[8,8,256,128]{3,2,1,0:T(8,128)} %bitcast.6), custom_call_target="tpu_custom_call" | custom-call | tf_op jit(solution)/shard_map/pallas_call | solution.py:445
  58.6 1.5 %copy.9 = f32[4,1,4096]{2,1,0:T(1,128)} copy(f32[4,1,4096]{2,1,0:T(1,128)} %bitcast.7) | data formatting | bytes 131072
